TPU v7x, 32 devices: a whole 2x2x4 slice. The times are simulated.
32 devices in a mesh: seq: 4 (over x, core), clip: 8 (over z, y).
Axes of the slice: x: 2, y: 2, z: 4, core: 2. Of those that a mesh axis runs over, the one named last changes fastest.
Arguments:
- patches: bfloat16 [64, 8, 64, 768], P('clip', None, 'seq'), may hold values from -6 to 6
- mask_index: int32 [64, 450], P('clip'), may hold values from 0 to 511, as said below
- mask_count: int32 [64], P('clip'), may hold values from 100 to 450, as said below
- cotangent: bfloat16 [64, 8, 64, 768], P('clip', None, 'seq'), may hold values from -6 to 6
- w_qkv: bfloat16 [768, 2304], P(('seq', 'clip')), may hold values from -0.3125 to 0.3125
- w_out: bfloat16 [768, 768], P(('seq', 'clip')), may hold values from -0.4375 to 0.4375
- mask_embed: bfloat16 [768], P(('seq', 'clip')), may hold values from -5 to 5
- gains: bfloat16 [2, 768], P(None, ('seq', 'clip')), may hold values from 0.5 to 1.5
- biases: bfloat16 [6, 768], P(None, ('seq', 'clip')), may hold values from -0.5 to 0.5
- w_up: bfloat16 [768, 3072], P(('seq', 'clip')), may hold values from -0.21875 to 0.21875
- w_down: bfloat16 [3072, 768], P(('seq', 'clip')), may hold values from -0.109375 to 0.109375
- up_bias: bfloat16 [3072], P(('seq', 'clip')), may hold values from -2.5 to 2.5
- avg_qkv: float32 [768, 2304], P(('seq', 'clip')), may hold values from -0.3125 to 0.3125
- avg_out: float32 [768, 768], P(('seq', 'clip')), may hold values from -0.4375 to 0.4375
- avg_mask: float32 [768], P(('seq', 'clip')), may hold values from -5 to 5
- avg_gains: float32 [2, 768], P(None, ('seq', 'clip')), may hold values from -1 to 1
- avg_biases: float32 [6, 768], P(None, ('seq', 'clip')), may hold values from -0.5 to 0.5
- avg_up: float32 [768, 3072], P(('seq', 'clip')), may hold values from -0.21875 to 0.21875
- avg_down: float32 [3072, 768], P(('seq', 'clip')), may hold values from -0.109375 to 0.109375
- avg_up_bias: float32 [3072], P(('seq', 'clip')), may hold values from -2.5 to 2.5
Outputs:
- activations: bfloat16 [64, 8, 64, 768], P('clip', None, 'seq')
- input_grad: bfloat16 [64, 8, 64, 768], P('clip', None, 'seq')
- grad_qkv: float32 [768, 2304], P(('seq', 'clip'))
- grad_out: float32 [768, 768], P(('seq', 'clip'))
- grad_mask: float32 [768], P(('seq', 'clip'))
- grad_gains: float32 [2, 768], P(None, ('seq', 'clip'))
- grad_biases: float32 [6, 768], P(None, ('seq', 'clip'))
- grad_up: float32 [768, 3072], P(('seq', 'clip'))
- grad_down: float32 [3072, 768], P(('seq', 'clip'))
- grad_up_bias: float32 [3072], P(('seq', 'clip'))
- new_qkv: float32 [768, 2304], P(('seq', 'clip'))
- new_out: float32 [768, 768], P(('seq', 'clip'))
- new_mask: float32 [768], P(('seq', 'clip'))
- new_gains: float32 [2, 768], P(None, ('seq', 'clip'))
- new_biases: float32 [6, 768], P(None, ('seq', 'clip'))
- new_up: float32 [768, 3072], P(('seq', 'clip'))
- new_down: float32 [3072, 768], P(('seq', 'clip'))
- new_up_bias: float32 [3072], P(('seq', 'clip'))
Inputs may be any that keep to these rules, and one draw needn't show every extreme that they name: `mask_index`: each row holds 450 different patch numbers of its clip; only its first mask_count entries are masked, the others are to be ignored. `mask_count`: some clip has exactly 450 masked patches in every draw.
All inputs are finite; a program needn't handle non-finite values.
Results may differ from a plain program's by a relative error of at most 0.015.
Values may be sent and summed in bfloat16 or wider, within the bound.
No kernel may reach another device: no remote copies, remote signals or barrier semaphores. Data moves between devices by JAX's collectives and lax.ppermute only.
A program may use at most 192 MiB of HBM per device.

v0:
```python
from functools import partial
import math
import jax
import jax.numpy as jnp
from jax import lax
from jax.sharding import PartitionSpec as P

H = 12
norm_eps = 1e-06


def layer_norm(hidden, gain_row, shift_row):
    center = hidden - jnp.mean(hidden, axis=-1, keepdims=True)
    spread = jnp.mean(center * center, axis=-1, keepdims=True)
    return center * lax.rsqrt(spread + norm_eps) * gain_row + shift_row


def exact_gelu(upper_rows):
    return jax.nn.gelu(upper_rows, approximate=False)


def row_product(left_side, right_side):
    return lax.dot_general(
        left_side, right_side, (((0,), (0,)), ((), ())), preferred_element_type=jnp.float32
    )


def back_product(left_side, right_side):
    return lax.dot_general(
        left_side, right_side, (((1,), (1,)), ((), ())), preferred_element_type=jnp.float32
    )


def split_heads(array_rows, head_count):
    clip_count, row_count, model_width = array_rows.shape
    return array_rows.reshape(clip_count, row_count, head_count, model_width // head_count)


def make_groups(array_rows, group_size):
    return array_rows.reshape(
        (array_rows.shape[0] // group_size, group_size) + array_rows.shape[1:]
    )


def attend_forward(operands, head_count, score_scale):
    queries, keys_all, values_all = operands
    clip_count, query_rows, model_width = queries.shape
    query_h = split_heads(queries, head_count)
    key_h = split_heads(keys_all, head_count)
    value_h = split_heads(values_all, head_count)
    scores = (
        jnp.einsum("cqhd,ckhd->chqk", query_h, key_h, preferred_element_type=jnp.float32)
        * score_scale
    )
    row_max = jnp.max(scores, axis=-1, keepdims=True)
    shifted = jnp.exp(scores - row_max)
    row_sum = jnp.sum(shifted, axis=-1, keepdims=True)
    attn_prob = shifted / row_sum
    mixed_rows = jnp.einsum(
        "chqk,ckhd->cqhd",
        attn_prob.astype(jnp.bfloat16),
        value_h,
        preferred_element_type=jnp.float32,
    )
    log_total = (row_max + jnp.log(row_sum))[..., 0]
    return (mixed_rows.reshape(clip_count, query_rows, model_width).astype(jnp.bfloat16), log_total)


def attend_backward(operands, head_count, score_scale):
    queries, keys_all, values_all, grad_mixed, log_total = operands
    clip_count, query_rows, model_width = queries.shape
    key_rows = keys_all.shape[1]
    query_h = split_heads(queries, head_count)
    key_h = split_heads(keys_all, head_count)
    value_h = split_heads(values_all, head_count)
    grad_heads = split_heads(grad_mixed, head_count)
    scores = (
        jnp.einsum("cqhd,ckhd->chqk", query_h, key_h, preferred_element_type=jnp.float32)
        * score_scale
    )
    attn_prob = jnp.exp(scores - log_total[..., None])
    grad_prob = jnp.einsum(
        "cqhd,ckhd->chqk", grad_heads, value_h, preferred_element_type=jnp.float32
    )
    inner_sum = jnp.sum(grad_prob * attn_prob, axis=-1, keepdims=True)
    grad_scores = (attn_prob * (grad_prob - inner_sum)).astype(jnp.bfloat16)
    grad_query = (
        jnp.einsum("chqk,ckhd->cqhd", grad_scores, key_h, preferred_element_type=jnp.float32)
        * score_scale
    )
    grad_key = (
        jnp.einsum("chqk,cqhd->ckhd", grad_scores, query_h, preferred_element_type=jnp.float32)
        * score_scale
    )
    grad_value = jnp.einsum(
        "chqk,cqhd->ckhd",
        attn_prob.astype(jnp.bfloat16),
        grad_heads,
        preferred_element_type=jnp.float32,
    )
    grad_query = grad_query.reshape(clip_count, query_rows, model_width).astype(jnp.bfloat16)
    grad_key = grad_key.reshape(clip_count, key_rows, model_width)
    grad_value = grad_value.reshape(clip_count, key_rows, model_width)
    return (grad_query, grad_key, grad_value)


def body(
    patches,
    mask_index,
    mask_count,
    cotangent,
    w_qkv,
    w_out,
    mask_embed,
    gains,
    biases,
    w_up,
    w_down,
    up_bias,
    avg_qkv,
    avg_out,
    avg_mask,
    avg_gains,
    avg_biases,
    avg_up,
    avg_down,
    avg_up_bias,
):
    clip_count, freq_rows, time_local, model_width = patches.shape
    seq_size = lax.axis_size("seq")
    time_total = time_local * seq_size
    length = freq_rows * time_total
    local_len = freq_rows * time_local
    row_total = clip_count * local_len
    head_count = H
    score_scale = 1.0 / math.sqrt(model_width // head_count)
    forward_fn = partial(attend_forward, head_count=head_count, score_scale=score_scale)
    backward_fn = partial(attend_backward, head_count=head_count, score_scale=score_scale)
    gathered = (
        lax.all_gather(w_qkv, ("seq", "clip"), axis=0, tiled=True),
        lax.all_gather(w_out, ("seq", "clip"), axis=0, tiled=True),
        lax.all_gather(mask_embed, ("seq", "clip"), axis=0, tiled=True),
        lax.all_gather(gains, ("seq", "clip"), axis=1, tiled=True),
        lax.all_gather(biases, ("seq", "clip"), axis=1, tiled=True),
        lax.all_gather(w_up, ("seq", "clip"), axis=0, tiled=True),
        lax.all_gather(w_down, ("seq", "clip"), axis=0, tiled=True),
        lax.all_gather(up_bias, ("seq", "clip"), axis=0, tiled=True),
    )
    full_qkv, full_out, full_mask, full_gains, full_biases, full_up, full_down, full_up_bias = (
        gathered
    )
    gain_rows = full_gains.astype(jnp.float32)
    bias_rows = full_biases.astype(jnp.float32)
    mask_vector = full_mask.astype(jnp.float32)
    up_shift = full_up_bias.astype(jnp.float32)
    freq_ids = lax.broadcasted_iota(jnp.int32, (freq_rows, time_local), 0)
    time_ids = (
        lax.broadcasted_iota(jnp.int32, (freq_rows, time_local), 1)
        + lax.axis_index("seq") * time_local
    )
    positions = (freq_ids * time_total + time_ids).reshape(local_len)
    slot_ids = lax.broadcasted_iota(jnp.int32, mask_index.shape, 1)
    slot_live = slot_ids < mask_count[:, None]
    slot_hits = (mask_index[:, :, None] == positions[None, None, :]) & slot_live[:, :, None]
    masked = jnp.any(slot_hits, axis=1).reshape(row_total, 1)
    fresh_rows = patches.reshape(row_total, model_width).astype(jnp.float32)
    start_rows = jnp.where(masked, mask_vector, fresh_rows)
    normed_one, norm_pull_one = jax.vjp(layer_norm, start_rows, gain_rows[0], bias_rows[0])
    normed_low = normed_one.astype(jnp.bfloat16)
    joined = jnp.dot(normed_low, full_qkv, preferred_element_type=jnp.float32)
    queries = (joined[:, :model_width] + bias_rows[1]).astype(jnp.bfloat16)
    keys_loc = joined[:, model_width : 2 * model_width].astype(jnp.bfloat16)
    values_loc = (joined[:, 2 * model_width :] + bias_rows[2]).astype(jnp.bfloat16)
    grid_shape = (clip_count, freq_rows, time_local, model_width)
    key_grid = keys_loc.reshape(grid_shape)
    value_grid = values_loc.reshape(grid_shape)
    key_all, value_all = (
        lax.all_gather(key_grid, "seq", axis=2, tiled=True),
        lax.all_gather(value_grid, "seq", axis=2, tiled=True),
    )
    group_size = math.gcd(clip_count, max(1, 512 // local_len))
    query_groups = make_groups(queries.reshape(clip_count, local_len, model_width), group_size)
    key_groups = make_groups(key_all.reshape(clip_count, length, model_width), group_size)
    value_groups = make_groups(value_all.reshape(clip_count, length, model_width), group_size)
    mixed_groups, log_groups = lax.map(forward_fn, (query_groups, key_groups, value_groups))
    mixed_flat = mixed_groups.reshape(row_total, model_width)
    middle = start_rows + (
        jnp.dot(mixed_flat, full_out, preferred_element_type=jnp.float32) + bias_rows[3]
    )
    normed_two, norm_pull_two = jax.vjp(layer_norm, middle, gain_rows[1], bias_rows[4])
    second_low = normed_two.astype(jnp.bfloat16)
    upper_rows = jnp.dot(second_low, full_up, preferred_element_type=jnp.float32) + up_shift
    active, gelu_pull = jax.vjp(exact_gelu, upper_rows)
    active_low = active.astype(jnp.bfloat16)
    final_rows = middle + (
        jnp.dot(active_low, full_down, preferred_element_type=jnp.float32) + bias_rows[5]
    )
    activations = final_rows.astype(jnp.bfloat16).reshape(patches.shape)
    grad_final = cotangent.reshape(row_total, model_width)
    grad_down_part = row_product(active_low, grad_final)
    grad_down_bias = jnp.sum(grad_final.astype(jnp.float32), axis=0)
    grad_active = back_product(grad_final, full_down)
    (grad_upper,) = gelu_pull(grad_active)
    grad_upper_low = grad_upper.astype(jnp.bfloat16)
    grad_up_part = row_product(second_low, grad_upper_low)
    grad_up_shift = jnp.sum(grad_upper_low.astype(jnp.float32), axis=0)
    grad_second = back_product(grad_upper_low, full_up)
    grad_mid_norm, grad_gain_two, grad_bias_two = norm_pull_two(grad_second)
    grad_middle = grad_final.astype(jnp.float32) + grad_mid_norm
    grad_branch = grad_middle.astype(jnp.bfloat16)
    grad_out_part = row_product(mixed_flat, grad_branch)
    grad_out_bias = jnp.sum(grad_branch.astype(jnp.float32), axis=0)
    grad_mixed = back_product(grad_branch, full_out).astype(jnp.bfloat16)
    grad_mixed_groups = make_groups(
        grad_mixed.reshape(clip_count, local_len, model_width), group_size
    )
    grad_query_groups, grad_key_groups, grad_value_groups = lax.map(
        backward_fn, (query_groups, key_groups, value_groups, grad_mixed_groups, log_groups)
    )
    grad_key_own, grad_value_own = (
        lax.psum_scatter(
            grad_key_groups.reshape(clip_count, freq_rows, time_total, model_width).astype(
                jnp.bfloat16
            ),
            "seq",
            scatter_dimension=2,
            tiled=True,
        ).astype(jnp.float32),
        lax.psum_scatter(
            grad_value_groups.reshape(clip_count, freq_rows, time_total, model_width).astype(
                jnp.bfloat16
            ),
            "seq",
            scatter_dimension=2,
            tiled=True,
        ).astype(jnp.float32),
    )
    grad_query_loc = grad_query_groups.reshape(row_total, model_width)
    grad_key_loc = grad_key_own.reshape(row_total, model_width).astype(jnp.bfloat16)
    grad_value_loc = grad_value_own.reshape(row_total, model_width).astype(jnp.bfloat16)
    grad_joined = jnp.concatenate([grad_query_loc, grad_key_loc, grad_value_loc], axis=1)
    grad_qkv_part = row_product(normed_low, grad_joined)
    grad_query_bias = jnp.sum(grad_query_loc.astype(jnp.float32), axis=0)
    grad_value_bias = jnp.sum(grad_value_loc.astype(jnp.float32), axis=0)
    grad_first = back_product(grad_joined, full_qkv)
    grad_start_norm, grad_gain_one, grad_bias_one = norm_pull_one(grad_first)
    grad_start = grad_middle + grad_start_norm
    input_grad = jnp.where(masked, 0.0, grad_start).astype(jnp.bfloat16).reshape(patches.shape)
    grad_mask_part = jnp.sum(jnp.where(masked, grad_start, 0.0), axis=0)
    grad_gain_part = jnp.stack([grad_gain_one, grad_gain_two])
    grad_bias_part = jnp.stack(
        [
            grad_bias_one,
            grad_query_bias,
            grad_value_bias,
            grad_out_bias,
            grad_bias_two,
            grad_down_bias,
        ]
    )
    summed = (
        lax.psum_scatter(grad_qkv_part, ("seq", "clip"), scatter_dimension=0, tiled=True),
        lax.psum_scatter(grad_out_part, ("seq", "clip"), scatter_dimension=0, tiled=True),
        lax.psum_scatter(grad_mask_part, ("seq", "clip"), scatter_dimension=0, tiled=True),
        lax.psum_scatter(grad_gain_part, ("seq", "clip"), scatter_dimension=1, tiled=True),
        lax.psum_scatter(grad_bias_part, ("seq", "clip"), scatter_dimension=1, tiled=True),
        lax.psum_scatter(grad_up_part, ("seq", "clip"), scatter_dimension=0, tiled=True),
        lax.psum_scatter(grad_down_part, ("seq", "clip"), scatter_dimension=0, tiled=True),
        lax.psum_scatter(grad_up_shift, ("seq", "clip"), scatter_dimension=0, tiled=True),
    )
    new_qkv = 0.9 * avg_qkv + 0.1 * w_qkv.astype(jnp.float32)
    new_out = 0.9 * avg_out + 0.1 * w_out.astype(jnp.float32)
    new_mask = 0.9 * avg_mask + 0.1 * mask_embed.astype(jnp.float32)
    new_gains = 0.9 * avg_gains + 0.1 * gains.astype(jnp.float32)
    new_biases = 0.9 * avg_biases + 0.1 * biases.astype(jnp.float32)
    new_up = 0.9 * avg_up + 0.1 * w_up.astype(jnp.float32)
    new_down = 0.9 * avg_down + 0.1 * w_down.astype(jnp.float32)
    new_up_bias = 0.9 * avg_up_bias + 0.1 * up_bias.astype(jnp.float32)
    return (
        activations,
        input_grad,
        summed[0],
        summed[1],
        summed[2],
        summed[3],
        summed[4],
        summed[5],
        summed[6],
        summed[7],
        new_qkv,
        new_out,
        new_mask,
        new_gains,
        new_biases,
        new_up,
        new_down,
        new_up_bias,
    )


def solution(mesh):
    placed = (
        P("clip", None, "seq", None),
        P("clip", None),
        P("clip"),
        P("clip", None, "seq", None),
        P(("seq", "clip"), None),
        P(("seq", "clip"), None),
        P(("seq", "clip")),
        P(None, ("seq", "clip")),
        P(None, ("seq", "clip")),
        P(("seq", "clip"), None),
        P(("seq", "clip"), None),
        P(("seq", "clip")),
        P(("seq", "clip"), None),
        P(("seq", "clip"), None),
        P(("seq", "clip")),
        P(None, ("seq", "clip")),
        P(None, ("seq", "clip")),
        P(("seq", "clip"), None),
        P(("seq", "clip"), None),
        P(("seq", "clip")),
    )
    return jax.shard_map(
        body,
        mesh=mesh,
        in_specs=placed,
        out_specs=(
            P("clip", None, "seq", None),
            P("clip", None, "seq", None),
            P(("seq", "clip"), None),
            P(("seq", "clip"), None),
            P(("seq", "clip")),
            P(None, ("seq", "clip")),
            P(None, ("seq", "clip")),
            P(("seq", "clip"), None),
            P(("seq", "clip"), None),
            P(("seq", "clip")),
            P(("seq", "clip"), None),
            P(("seq", "clip"), None),
            P(("seq", "clip")),
            P(None, ("seq", "clip")),
            P(None, ("seq", "clip")),
            P(("seq", "clip"), None),
            P(("seq", "clip"), None),
            P(("seq", "clip")),
        ),
        check_vma=False,
    )
```

profile of v0, /device:TPU:0, one launch (start us, length us, event | category | flops | bytes accessed | tf_op | source)
XLA Modules:
  0.0 1272.0 jit_solution(1368373145277587235)
XLA Ops:
  9.9 42.7 %all-reduce.7 = (bf16[768]{0:T(1024)(128)(2,1)S(1)}, bf16[3072]{0:T(1024)(128)(2,1)S(1)}) all-reduce(bf16[768]{0:T(1024)(128)(2,1)S(1)} %dynamic-update-slice, bf16[3072]{0:T(1024)(128)(2,1)S(1)} %dynamic-update-slice.1), channel_id=1, replica_groups=mesh['seq'=4,'clip'=8] {'seq','clip'}, use_global_device_ids=true, to_apply=%add | all-reduce | flops 3840 | bytes 15360
  52.6 65.9 %all-gather = bf16[32,24,2]{1,2,0:T(2,128)(2,1)S(1)} all-gather(bf16[1,24,2]{1,2,0:T(2,128)(2,1)} %bitcast.197), channel_id=1, replica_groups=mesh['seq'=4,'clip'=8] {'seq','clip'}, dimensions={0}, use_global_device_ids=true | all-gather | bytes 3168 | tf_op jit(solution)/shard_map/all_gather | solution.py:143
  118.8 63.9 %all-gather.1 = bf16[32,24,6]{1,2,0:T(8,128)(2,1)S(1)} all-gather(bf16[1,24,6]{1,2,0:T(8,128)(2,1)} %bitcast.196), channel_id=1, replica_groups=mesh['seq'=4,'clip'=8] {'seq','clip'}, dimensions={0}, use_global_device_ids=true | all-gather | bytes 9504 | tf_op jit(solution)/shard_map/all_gather | solution.py:144
  192.0 6.4 fusion.35
  198.4 3.6 copy-done.16
  203.4 4.5 fusion.16
  212.2 35.7 %all-gather.13.cloned.1.call-done = bf16[8,8,64,768]{3,2,1,0:T(8,128)(2,1)} async-done(((bf16[8,8,16,768]{3,2,1,0:T(8,128)(2,1)}), bf16[8,8,64,768]{3,2,1,0:T(8,128)(2,1)}) %all-gather.13.cloned.1.call-update) | async-done | bytes 6291472 | tf_op jit(solution)/shard_map/all_gather | solution.py:178
  247.9 8.7 copy.90
  256.5 39.8 %all-gather.11.cloned.1.call-done = bf16[8,8,64,768]{3,2,1,0:T(8,128)(2,1)} async-done(((bf16[8,8,16,768]{3,2,1,0:T(8,128)(2,1)}), bf16[8,8,64,768]{3,2,1,0:T(8,128)(2,1)}) %all-gather.11.cloned.1.call-update) | async-done | bytes 6291472 | tf_op jit(solution)/shard_map/all_gather | solution.py:179
  296.4 8.6 copy.88
  305.0 30.4 %while.26 = (s32[]{:T(128)}, bf16[2,4,128,768]{3,2,1,0:T(8,128)(2,1)S(1)}, f32[2,4,12,128]{3,2,1,0:T(8,128)S(1)}, bf16[2,4,512,768]{2,3,1,0:T(8,128)(2,1)}, bf16...) while((s32[]{:T(128)}, bf16[2,4,128,768]{3,2,1,0:T(8,128)(2,1)S(1)}, ...), condition=%wide.region_6.7_spmd, body=%wide.region_3.6_spmd.sunk | while | flops 834004992 | bytes 63135844 | solution.py:185
  314.6 5.2 fusion.91
  329.8 5.2 fusion.91
  335.4 17.9 %all-gather.15.cloned.1.call-done = bf16[768,768]{1,0:T(8,128)(2,1)} async-done(((bf16[24,768]{1,0:T(8,128)(2,1)}), bf16[768,768]{1,0:T(8,128)(2,1)}) %all-gather.15.cloned.1.call-update) | async-done | bytes 1179664 | tf_op jit(solution)/shard_map/all_gather | solution.py:141
  353.3 3.9 fusion.33
  357.8 60.8 %all-gather.17.cloned.1.call-done = bf16[768,3072]{1,0:T(8,128)(2,1)} async-done(((bf16[24,3072]{1,0:T(8,128)(2,1)}), bf16[768,3072]{1,0:T(8,128)(2,1)}) %all-gather.17.cloned.1.call-update) | async-done | bytes 4718608 | tf_op jit(solution)/shard_map/all_gather | solution.py:145
  418.5 35.8 %multiply_convert_fusion.2 = (bf16[1024,3072]{1,0:T(8,128)(2,1)}, f32[1024,3072]{1,0:T(8,128)}, f32[1024,3072]{1,0:T(8,128)}) fusion(f32[3072]{0:T(1024)S(1)} %copy-done.51, bf16[768,3072]{1,0:T(8,128)(2,1)} %all-gather.17.cloned.1.call-done, f32[1024,768]{1,0:T(8,128)S(1)} %get-tuple-element.251, f32[768]{0:T(1024)S(1)} %copy-done.35, ...), kind=kOutput, calls=%fused_computation.34 | convolution fusion | flops 5043388416 | bytes 39348224 | tf_op jit(solution)/shard_map/dot_general | solution.py:192
  454.3 28.8 %all-gather.19.cloned.1.call-done = bf16[3072,768]{1,0:T(8,128)(2,1)} async-done(((bf16[96,768]{1,0:T(8,128)(2,1)}), bf16[3072,768]{1,0:T(8,128)(2,1)}) %all-gather.19.cloned.1.call-update) | async-done | bytes 4718608 | tf_op jit(solution)/shard_map/all_gather | solution.py:146
  483.1 19.3 %convert_reduce_fusion = (f32[3072]{0:T(1024)}, bf16[1024,3072]{1,0:T(8,128)(2,1)}) fusion(f32[1024,3072]{1,0:T(8,128)} %get-tuple-element.237, bf16[1024,768]{1,0:T(8,128)(2,1)} %bitcast.175, bf16[3072,768]{1,0:T(8,128)(2,1)} %all-gather.19.cloned.1.call-done, f32[1024,3072]{1,0:T(8,128)} %get-tuple-element.252, f32[3072]{0:T(1024)S(1)} %copy-done.51), kind=kOutput, calls=%fused_computation.32 | convolution fusion | flops 4885312512 | bytes 37773312 | tf_op jit(solution)/shard_map/dot_general | solution.py:29
  502.5 9.8 multiply_reduce_fusion.2
  518.5 115.8 %while.27 = (s32[]{:T(128)}, bf16[2,4,128,768]{2,3,1,0:T(8,128)(2,1)}, bf16[2,4,512,768]{3,2,1,0:T(8,128)(2,1)}, bf16[2,4,512,768]{3,2,1,0:T(8,128)(2,1)}, bf16[...) while((s32[]{:T(128)}, ...), condition=%wide.region_13.14_spmd, body=%wide.region_11.13_spmd.sunk | while | flops 2054940672 | bytes 306094400 | solution.py:217
  522.2 4.1 constant_dynamic-slice_fusion.20
  529.5 5.2 fusion.103
  534.9 4.7 copy.134
  539.6 12.5 multiply_reduce_fusion.11
  552.1 6.6 multiply_convert_fusion.5
  564.6 4.8 copy.135
  571.5 4.9 constant_dynamic-update-slice_fusion.9
  580.0 4.1 constant_dynamic-slice_fusion.20
  587.3 5.2 fusion.103
  592.7 4.7 copy.134
  597.4 12.5 multiply_reduce_fusion.11
  609.9 6.6 multiply_convert_fusion.5
  622.4 4.8 copy.135
  629.3 5.0 constant_dynamic-update-slice_fusion.9
  635.2 4.9 fusion.36
  640.2 12.3 fusion.27
  652.6 10.7 fusion.37
  666.1 24.6 %reduce-scatter.9.cloned.1.call-done = bf16[8,8,16,768]{3,2,1,0:T(8,128)(2,1)} async-done(((bf16[8,8,64,768]{3,2,1,0:T(8,128)(2,1)}), bf16[8,8,16,768]{3,2,1,0:T(8,128)(2,1)}) %reduce-scatter.9.cloned.1.call-update) | async-done | bytes 1572880 | tf_op jit(solution)/shard_map/reduce_scatter | solution.py:221
  690.7 60.5 %reduce-scatter.11.cloned.1.call-done = bf16[8,8,16,768]{3,2,1,0:T(8,128)(2,1)} async-done(((bf16[8,8,64,768]{3,2,1,0:T(8,128)(2,1)}), bf16[8,8,16,768]{3,2,1,0:T(8,128)(2,1)}) %reduce-scatter.11.cloned.1.call-update) | async-done | bytes 1572880 | tf_op jit(solution)/shard_map/reduce_scatter | solution.py:229
  751.1 9.6 fusion.22
  774.4 9.6 add_convert_fusion.1
  784.5 5.8 multiply_reduce_fusion.3
  796.0 40.3 %all-reduce.6 = (f32[768]{0:T(1024)S(1)}, f32[2,768]{1,0:T(2,128)S(1)}, f32[6,768]{1,0:T(8,128)S(1)}, f32[3072]{0:T(1024)S(1)}) all-reduce(f32[768]{0:T(1024)S(1)} %get-tuple-element.248, f32[2,768]{1,0:T(2,128)S(1)} %pad_maximum_fusion.3, f32[6,768]{1,0:T(8,128)S(1)} %stack.27, ...), channel_id=6, replica_groups=mesh['seq'=4,'clip'=8] {'seq','clip'}, use_global_device_ids=true, to_apply=%region_21.22.clone | all-reduce | flops 9984 | bytes 79872
  838.8 18.1 %reduce-scatter.15.cloned.1.call-done = f32[24,768]{1,0:T(8,128)} async-done(((f32[768,768]{1,0:T(8,128)}), f32[24,768]{1,0:T(8,128)}) %reduce-scatter.15.cloned.1.call-update) | async-done | bytes 73744 | tf_op jit(solution)/shard_map/reduce_scatter | solution.py:263
  856.9 141.5 %reduce-scatter.17.cloned.1.call-done = f32[24,3072]{1,0:T(8,128)} async-done(((f32[768,3072]{1,0:T(8,128)}), f32[24,3072]{1,0:T(8,128)}) %reduce-scatter.17.cloned.1.call-update) | async-done | bytes 294928 | tf_op jit(solution)/shard_map/reduce_scatter | solution.py:267
  998.4 141.7 %reduce-scatter.19.cloned.1.call-done = f32[96,768]{1,0:T(8,128)} async-done(((f32[3072,768]{1,0:T(8,128)}), f32[96,768]{1,0:T(8,128)}) %reduce-scatter.19.cloned.1.call-update) | async-done | bytes 294928 | tf_op jit(solution)/shard_map/reduce_scatter | solution.py:268
  1140.1 124.7 %reduce-scatter.13.cloned.1.call-done = f32[24,2304]{1,0:T(8,128)} async-done(((f32[768,2304]{1,0:T(8,128)}), f32[24,2304]{1,0:T(8,128)}) %reduce-scatter.13.cloned.1.call-update) | async-done | bytes 221200 | tf_op jit(solution)/shard_map/reduce_scatter | solution.py:262
  (269 shorter events, 99.8 us)
Async XLA Ops:
  7.2 181.5 %copy-start.11 = (bf16[8,8,16,768]{3,2,1,0:T(8,128)(2,1)S(1)}, bf16[8,8,16,768]{3,2,1,0:T(8,128)(2,1)}, u32[]{:S(2)}) copy-start(bf16[8,8,16,768]{3,2,1,0:T(8,128)(2,1)} %param.24) | copy-start | bytes 4718596
  7.2 184.8 %all-gather.9.cloned.1.call-start = ((), (), s32[]{:S(2)}) async-start(), calls=%async_computation.6 | async-start | bytes 3649536 | tf_op jit(solution)/shard_map/all_gather | solution.py:140
  7.9 239.9 %all-gather.13.cloned.1.call-start = ((), (), s32[]{:S(2)}) async-start(), calls=%async_computation.8 | async-start | bytes 7864320 | tf_op jit(solution)/shard_map/all_gather | solution.py:178
  52.6 139.4 %copy-start.30 = (f32[768]{0:T(1024)}, f32[768]{0:T(1024)S(1)}, u32[]{:S(2)}) copy-start(f32[768]{0:T(1024)S(1)} %convert_element_type.162) | copy-start | bytes 9220
  188.7 9.7 copy-start.37
  203.4 93.0 %all-gather.11.cloned.1.call-start = ((), (), s32[]{:S(2)}) async-start(), calls=%async_computation.7 | async-start | bytes 7864320 | tf_op jit(solution)/shard_map/all_gather | solution.py:179
  208.0 145.3 %all-gather.15.cloned.1.call-start = ((), (), s32[]{:S(2)}) async-start(), calls=%async_computation.9 | async-start | bytes 1216512 | tf_op jit(solution)/shard_map/all_gather | solution.py:141
  208.5 210.0 %all-gather.17.cloned.1.call-start = ((), (), s32[]{:S(2)}) async-start(), calls=%async_computation.10 | async-start | bytes 4866048 | tf_op jit(solution)/shard_map/all_gather | solution.py:145
  209.1 274.0 %all-gather.19.cloned.1.call-start = ((), (), s32[]{:S(2)}) async-start(), calls=%async_computation.11 | async-start | bytes 4866048 | tf_op jit(solution)/shard_map/all_gather | solution.py:146
  209.7 481.0 %reduce-scatter.9.cloned.1.call-start = ((), (), s32[]{:S(2)}) async-start(), calls=%async_computation.12 | async-start | bytes 7864320 | tf_op jit(solution)/shard_map/reduce_scatter | solution.py:221
  305.0 48.3 %copy-start.31 = (f32[768]{0:T(1024)S(1)}, f32[768]{0:T(1024)}, u32[]{:S(2)}) copy-start(f32[768]{0:T(1024)} %copy-done.30) | copy-start | bytes 9220
  305.0 48.3 %copy-start.48 = (pred[8,128]{1,0:T(8,128)(4,1)S(1)}, pred[8,128]{1,0:T(8,128)(4,1)}, u32[]{:S(2)}) copy-start(pred[8,128]{1,0:T(8,128)(4,1)} %copy-done.47) | copy-start | bytes 3076
  305.0 48.3 %copy-start.57 = (f32[768]{0:T(1024)S(1)}, f32[768]{0:T(1024)}, u32[]{:S(2)}) copy-start(f32[768]{0:T(1024)} %get-tuple-element.188) | copy-start | bytes 9220
  335.4 17.9 %copy-start.60 = (bf16[2,4,128,768]{3,2,1,0:T(8,128)(2,1)}, bf16[2,4,128,768]{3,2,1,0:T(8,128)(2,1)S(1)}, u32[]{:S(2)}) copy-start(bf16[2,4,128,768]{3,2,1,0:T(8,128)(2,1)S(1)} %get-tuple-element.100) | copy-start | bytes 4718596
  357.2 155.1 %copy-start.7 = (f32[1024,768]{1,0:T(8,128)}, f32[1024,768]{1,0:T(8,128)S(1)}, u32[]{:S(2)}) copy-start(f32[1024,768]{1,0:T(8,128)S(1)} %get-tuple-element.251) | copy-start | bytes 9437188
  357.2 61.3 %copy-start.33 = (f32[768]{0:T(1024)S(1)}, f32[768]{0:T(1024)}, u32[]{:S(2)}) copy-start(f32[768]{0:T(1024)} %get-tuple-element.192) | copy-start | bytes 9220
  357.2 61.3 %copy-start.35 = (f32[768]{0:T(1024)S(1)}, f32[768]{0:T(1024)}, u32[]{:S(2)}) copy-start(f32[768]{0:T(1024)} %get-tuple-element.187) | copy-start | bytes 9220
  357.2 61.3 %copy-start.51 = (f32[3072]{0:T(1024)S(1)}, f32[3072]{0:T(1024)}, u32[]{:S(2)}) copy-start(f32[3072]{0:T(1024)} %convert_element_type.172) | copy-start | bytes 36868
  357.2 155.0 %copy-start.25 = (f32[1024]{0:T(1024)}, f32[1024]{0:T(1024)S(1)}, u32[]{:S(2)}) copy-start(f32[1024]{0:T(1024)S(1)} %broadcast_multiply_fusion.2) | copy-start | bytes 12292
  357.7 154.5 %copy-start.28 = (f32[1024]{0:T(1024)}, f32[1024]{0:T(1024)S(1)}, u32[]{:S(2)}) copy-start(f32[1024]{0:T(1024)S(1)} %fusion.24) | copy-start | bytes 12292
  539.6 12.5 copy-start.1
  564.6 6.9 copy-start.2
  597.4 12.5 copy-start.1
  622.4 6.9 copy-start.2
  634.3 116.8 %reduce-scatter.11.cloned.1.call-start = ((), (), s32[]{:S(2)}) async-start(), calls=%async_computation.13 | async-start | bytes 7864320 | tf_op jit(solution)/shard_map/reduce_scatter | solution.py:229
  635.1 221.7 %reduce-scatter.15.cloned.1.call-start = ((), (), s32[]{:S(2)}) async-start(), calls=%async_computation.15 | async-start | bytes 2433024 | tf_op jit(solution)/shard_map/reduce_scatter | solution.py:263
  640.1 358.3 %reduce-scatter.17.cloned.1.call-start = ((), (), s32[]{:S(2)}) async-start(), calls=%async_computation.16 | async-start | bytes 9732096 | tf_op jit(solution)/shard_map/reduce_scatter | solution.py:267
  652.5 487.6 %reduce-scatter.19.cloned.1.call-start = ((), (), s32[]{:S(2)}) async-start(), calls=%async_computation.17 | async-start | bytes 9732096 | tf_op jit(solution)/shard_map/reduce_scatter | solution.py:268
  663.3 601.5 %reduce-scatter.13.cloned.1.call-start = ((), (), s32[]{:S(2)}) async-start(), calls=%async_computation.14 | async-start | bytes 7299072 | tf_op jit(solution)/shard_map/reduce_scatter | solution.py:262
  760.7 9.0 copy-start.22
  760.7 10.8 copy-start.24
  760.8 12.4 copy-start.23
  760.8 13.2 %copy-start.50 = (f32[768]{0:T(1024)S(1)}, f32[768]{0:T(1024)}, u32[]{:S(2)}) copy-start(f32[768]{0:T(1024)} %get-tuple-element.230) | copy-start | bytes 9220
  760.8 12.4 copy-start.27
  760.8 13.1 %copy-start.55 = (f32[768]{0:T(1024)S(1)}, f32[768]{0:T(1024)}, u32[]{:S(2)}) copy-start(f32[768]{0:T(1024)} %get-tuple-element.180) | copy-start | bytes 9220
  760.8 13.1 %copy-start.54 = (f32[768]{0:T(1024)S(1)}, f32[768]{0:T(1024)}, u32[]{:S(2)}) copy-start(f32[768]{0:T(1024)} %get-tuple-element.184) | copy-start | bytes 9220
  760.8 13.2 %copy-start.17 = (bf16[2,4,128,768]{2,3,1,0:T(8,128)(2,1)S(1)}, bf16[2,4,128,768]{2,3,1,0:T(8,128)(2,1)}, u32[]{:S(2)}) copy-start(bf16[2,4,128,768]{2,3,1,0:T(8,128)(2,1)} %get-tuple-element.102) | copy-start | bytes 4718596
  760.8 13.4 %copy-start.56 = (f32[768]{0:T(1024)S(1)}, f32[768]{0:T(1024)}, u32[]{:S(2)}) copy-start(f32[768]{0:T(1024)} %get-tuple-element.186) | copy-start | bytes 9220
  774.3 9.7 copy-start.19
  774.3 10.0 copy-start.12
  774.3 10.0 copy-start.20
  774.3 10.0 copy-start.32
  774.3 10.0 copy-start.38
  774.4 10.0 copy-start.40
  774.4 10.0 copy-start.42
  774.4 10.0 copy-start.49
  774.4 10.0 copy-start.58
  774.4 10.0 copy-start.59
  (33 other events, 125.9 us)
Sparse Core Ops, SparseCore 0:
  10.9 62.7 all-gather.8
  203.5 44.3 all-gather.12
  250.0 46.3 all-gather.10
  299.2 54.0 all-gather.14
  356.1 62.3 all-gather.16
  421.3 61.8 all-gather.18
  634.4 56.1 reduce-scatter.8
  693.2 57.8 reduce-scatter.10
  757.0 99.8 reduce-scatter.14
  863.2 135.1 reduce-scatter.16
  1004.9 135.1 reduce-scatter.18
  1146.2 118.5 reduce-scatter.12
where the time goes:
time: 1280 us; the launch traced here: 1270 us
  waiting for transfers between devices  697 us (54%)
  blocking collectives  213 us (17%)
  matrix products  196 us (15%)
  local copies, waits for them, and re-layouts  96.9 us (8%)
  other arithmetic  52.7 us (4%)
  between operations  15.5 us (1%)
    reduce_scatter x1, waiting for transfers between devices, body(): lax.psum_scatter(grad_down_part, ('seq', 'clip'), scatter_dimension=0, ti...  142 us
    reduce_scatter x1, waiting for transfers between devices, body(): lax.psum_scatter(grad_up_part, ('seq', 'clip'), scatter_dimension=0, tile...  142 us
    reduce_scatter x1, waiting for transfers between devices, body(): lax.psum_scatter(grad_qkv_part, ('seq', 'clip'), scatter_dimension=0, til...  125 us
    unnamed x2, blocking collectives  83 us
    all_gather x1, blocking collectives, body(): lax.all_gather(gains, ('seq', 'clip'), axis=1, tiled=True)  65.9 us
    all_gather x1, blocking collectives, body(): lax.all_gather(biases, ('seq', 'clip'), axis=1, tiled=True)  63.9 us
    all_gather x1, waiting for transfers between devices, body(): lax.all_gather(w_up, ('seq', 'clip'), axis=0, tiled=True)  60.8 us
    reduce_scatter x1, waiting for transfers between devices, body(): lax.psum_scatter(grad_value_groups.reshape(clip_count, freq_rows, time_to...  60.5 us
  transfers between devices with their start and end apart: 12, of which 11 were waited for; matrix products, arithmetic and copies ran while one was open for 14% of the time, Pallas kernels for 0%

commit v1 on v0

--- a/solution.py
+++ b/solution.py
@@ -7,6 +7,24 @@
 
 H = 12
 norm_eps = 1e-06
+
+
+def gather_around(shard, axis, dim):
+    ways, here, turn = (lax.axis_size(axis), lax.axis_index(axis), shard.shape[dim])
+    shape = [n * ways if d == dim else n for d, n in enumerate(shard.shape)]
+    full = lax.dynamic_update_slice_in_dim(
+        jnp.zeros(shape, shard.dtype), shard, here * turn, axis=dim
+    )
+    going_up = going_down = shard
+    for far in range(1, ways // 2 + 1):
+        going_up = lax.ppermute(going_up, axis, [(d, (d + 1) % ways) for d in range(ways)])
+        full = lax.dynamic_update_slice_in_dim(full, going_up, (here - far) % ways * turn, axis=dim)
+        if 2 * far < ways:
+            going_down = lax.ppermute(going_down, axis, [(d, (d - 1) % ways) for d in range(ways)])
+            full = lax.dynamic_update_slice_in_dim(
+                full, going_down, (here + far) % ways * turn, axis=dim
+            )
+    return full
 
 
 def layer_norm(hidden, gain_row, shift_row):
@@ -175,7 +193,7 @@
     key_grid = keys_loc.reshape(grid_shape)
     value_grid = values_loc.reshape(grid_shape)
     key_all, value_all = (
-        lax.all_gather(key_grid, "seq", axis=2, tiled=True),
+        gather_around(key_grid, "seq", 2),
         lax.all_gather(value_grid, "seq", axis=2, tiled=True),
     )
     group_size = math.gcd(clip_count, max(1, 512 // local_len))

time: 1280 us -> 1260 us (0.984)
  waiting for transfers between devices: 697 us -> 659 us
  local copies, waits for them, and re-layouts: 96.9 us -> 110 us
    ppermute x0 -> x3, waiting for transfers between devices: none -> 66.7 us  [the longest x2 66.7 us: gather_around(): lax.ppermute(going_up, axis, [(d, (d + 1) % ways) for d in range(ways)])]
    all_gather x1, waiting for transfers between devices: 39.8 us -> 0.01 us  [body(): lax.all_gather(value_grid, 'seq', axis=2, tiled=True)]
    all_gather x1 -> x0, waiting for transfers between devices: 35.7 us -> none  [body(): lax.all_gather(key_grid, 'seq', axis=2, tiled=True)]
    all_gather x1, waiting for transfers between devices: 17.9 us -> 0.02 us  [body(): lax.all_gather(w_out, ('seq', 'clip'), axis=0, tiled=True)]
  transfers between devices with their start and end apart: 12 -> 14, of which waited for: 11 -> 10; matrix products, arithmetic and copies ran while one was open for 14% -> 16% of each run, Pallas kernels for 0% -> 0%
where the time goes in v1:
time: 1260 us; the launch traced here: 1250 us
  waiting for transfers between devices  659 us (52%)
  blocking collectives  213 us (17%)
  matrix products  196 us (16%)
  local copies, waits for them, and re-layouts  110 us (9%)
  other arithmetic  50.4 us (4%)
  between operations  15.2 us (1%)
    reduce_scatter x1, waiting for transfers between devices, body(): lax.psum_scatter(grad_up_part, ('seq', 'clip'), scatter_dimension=0, tile...  142 us
    reduce_scatter x1, waiting for transfers between devices, body(): lax.psum_scatter(grad_down_part, ('seq', 'clip'), scatter_dimension=0, ti...  141 us
    reduce_scatter x1, waiting for transfers between devices, body(): lax.psum_scatter(grad_qkv_part, ('seq', 'clip'), scatter_dimension=0, til...  125 us
    unnamed x2, blocking collectives  83 us
    ppermute x2, waiting for transfers between devices, gather_around(): lax.ppermute(going_up, axis, [(d, (d + 1) % ways) for d in range(ways)])  66.7 us
    all_gather x1, blocking collectives, body(): lax.all_gather(gains, ('seq', 'clip'), axis=1, tiled=True)  65.9 us
    all_gather x1, blocking collectives, body(): lax.all_gather(biases, ('seq', 'clip'), axis=1, tiled=True)  63.9 us
    reduce_scatter x1, waiting for transfers between devices, body(): lax.psum_scatter(grad_value_groups.reshape(clip_count, freq_rows, time_to...  60.5 us
  transfers between devices with their start and end apart: 14, of which 10 were waited for; matrix products, arithmetic and copies ran while one was open for 16% of the time, Pallas kernels for 0%

profile of v1, /device:TPU:0, one launch (start us, length us, event | category | flops | bytes accessed | tf_op | source)
XLA Modules:
  0.0 1252.2 jit_solution(16342992711686398186)
XLA Ops:
  9.9 42.7 %all-reduce.7 = (bf16[768]{0:T(1024)(128)(2,1)S(1)}, bf16[3072]{0:T(1024)(128)(2,1)S(1)}) all-reduce(bf16[768]{0:T(1024)(128)(2,1)S(1)} %dynamic-update-slice, bf16[3072]{0:T(1024)(128)(2,1)S(1)} %dynamic-update-slice.1), channel_id=1, replica_groups=mesh['seq'=4,'clip'=8] {'seq','clip'}, use_global_device_ids=true, to_apply=%add | all-reduce | flops 3840 | bytes 15360
  52.6 65.9 %all-gather = bf16[32,24,2]{1,2,0:T(2,128)(2,1)S(1)} all-gather(bf16[1,24,2]{1,2,0:T(2,128)(2,1)} %bitcast.198), channel_id=1, replica_groups=mesh['seq'=4,'clip'=8] {'seq','clip'}, dimensions={0}, use_global_device_ids=true | all-gather | bytes 3168 | tf_op jit(solution)/shard_map/all_gather | solution.py:161
  118.8 63.9 %all-gather.1 = bf16[32,24,6]{1,2,0:T(8,128)(2,1)S(1)} all-gather(bf16[1,24,6]{1,2,0:T(8,128)(2,1)} %bitcast.197), channel_id=1, replica_groups=mesh['seq'=4,'clip'=8] {'seq','clip'}, dimensions={0}, use_global_device_ids=true | all-gather | bytes 9504 | tf_op jit(solution)/shard_map/all_gather | solution.py:162
  192.0 6.4 fusion.35
  207.8 61.1 %collective-permute-done = bf16[8,8,16,768]{3,2,1,0:T(8,128)(2,1)} collective-permute-done((bf16[8,8,16,768]{3,2,1,0:T(8,128)(2,1)S(1)}, bf16[8,8,16,768]{3,2,1,0:T(8,128)(2,1)}, u32[]{:S(2)}, u32[]{:S(2)}) %collective-permute-start) | collective-permute-done | bytes 1572896 | tf_op jit(solution)/shard_map/ppermute | solution.py:20
  268.8 6.4 collective-permute-start.2
  277.8 3.4 broadcast_in_dim.87
  287.9 5.7 collective-permute-done.2
  296.3 8.7 copy.93
  305.0 8.7 copy.91
  313.8 30.4 %while.26 = (s32[]{:T(128)}, bf16[2,4,128,768]{3,2,1,0:T(8,128)(2,1)S(1)}, f32[2,4,12,128]{3,2,1,0:T(8,128)S(1)}, bf16[2,4,512,768]{2,3,1,0:T(8,128)(2,1)}, bf16...) while((s32[]{:T(128)}, bf16[2,4,128,768]{3,2,1,0:T(8,128)(2,1)S(1)}, ...), condition=%wide.region_6.7_spmd, body=%wide.region_3.6_spmd.sunk | while | flops 834004992 | bytes 63135844 | solution.py:203
  323.3 5.2 fusion.91
  330.1 3.3 constant_dynamic-slice_fusion.15
  338.5 5.2 fusion.91
  345.3 3.9 fusion.33
  349.7 49.6 %all-gather.14.cloned.1.call-done = bf16[768,3072]{1,0:T(8,128)(2,1)} async-done(((bf16[24,3072]{1,0:T(8,128)(2,1)}), bf16[768,3072]{1,0:T(8,128)(2,1)}) %all-gather.14.cloned.1.call-update) | async-done | bytes 4718608 | tf_op jit(solution)/shard_map/all_gather | solution.py:163
  399.4 36.2 %multiply_convert_fusion.2 = (bf16[1024,3072]{1,0:T(8,128)(2,1)}, f32[1024,3072]{1,0:T(8,128)}, f32[1024,3072]{1,0:T(8,128)}) fusion(f32[3072]{0:T(1024)S(1)} %copy-done.51, bf16[768,3072]{1,0:T(8,128)(2,1)} %all-gather.14.cloned.1.call-done, f32[1024,768]{1,0:T(8,128)S(1)} %get-tuple-element.251, f32[768]{0:T(1024)S(1)} %copy-done.35, ...), kind=kOutput, calls=%fused_computation.34 | convolution fusion | flops 5043388416 | bytes 39348224 | tf_op jit(solution)/shard_map/dot_general | solution.py:210
  435.6 28.5 %all-gather.16.cloned.1.call-done = bf16[3072,768]{1,0:T(8,128)(2,1)} async-done(((bf16[96,768]{1,0:T(8,128)(2,1)}), bf16[3072,768]{1,0:T(8,128)(2,1)}) %all-gather.16.cloned.1.call-update) | async-done | bytes 4718608 | tf_op jit(solution)/shard_map/all_gather | solution.py:164
  464.1 18.7 %convert_reduce_fusion = (f32[3072]{0:T(1024)}, bf16[1024,3072]{1,0:T(8,128)(2,1)}) fusion(f32[1024,3072]{1,0:T(8,128)} %get-tuple-element.237, bf16[1024,768]{1,0:T(8,128)(2,1)} %bitcast.175, bf16[3072,768]{1,0:T(8,128)(2,1)} %all-gather.16.cloned.1.call-done, f32[1024,3072]{1,0:T(8,128)} %get-tuple-element.252, f32[3072]{0:T(1024)S(1)} %copy-done.51), kind=kOutput, calls=%fused_computation.32 | convolution fusion | flops 4885312512 | bytes 37773312 | tf_op jit(solution)/shard_map/dot_general | solution.py:47
  482.8 9.8 multiply_reduce_fusion.2
  498.8 115.8 %while.27 = (s32[]{:T(128)}, bf16[2,4,128,768]{2,3,1,0:T(8,128)(2,1)}, bf16[2,4,512,768]{3,2,1,0:T(8,128)(2,1)}, bf16[2,4,512,768]{3,2,1,0:T(8,128)(2,1)}, bf16[...) while((s32[]{:T(128)}, ...), condition=%wide.region_13.14_spmd, body=%wide.region_11.13_spmd.sunk | while | flops 2054940672 | bytes 306094400 | solution.py:235
  502.6 4.1 constant_dynamic-slice_fusion.20
  509.8 5.2 fusion.103
  515.2 4.7 copy.137
  520.0 12.5 multiply_reduce_fusion.11
  532.5 6.6 multiply_convert_fusion.5
  545.0 4.8 copy.138
  551.9 4.9 constant_dynamic-update-slice_fusion.13
  560.4 4.1 constant_dynamic-slice_fusion.20
  567.6 5.2 fusion.103
  573.0 4.7 copy.137
  577.8 12.5 multiply_reduce_fusion.11
  590.3 6.6 multiply_convert_fusion.5
  602.8 4.8 copy.138
  609.7 5.0 constant_dynamic-update-slice_fusion.13
  615.5 4.9 fusion.36
  620.5 12.3 fusion.27
  632.9 10.7 fusion.37
  646.4 24.6 %reduce-scatter.9.cloned.1.call-done = bf16[8,8,16,768]{3,2,1,0:T(8,128)(2,1)} async-done(((bf16[8,8,64,768]{3,2,1,0:T(8,128)(2,1)}), bf16[8,8,16,768]{3,2,1,0:T(8,128)(2,1)}) %reduce-scatter.9.cloned.1.call-update) | async-done | bytes 1572880 | tf_op jit(solution)/shard_map/reduce_scatter | solution.py:239
  671.0 60.5 %reduce-scatter.11.cloned.1.call-done = bf16[8,8,16,768]{3,2,1,0:T(8,128)(2,1)} async-done(((bf16[8,8,64,768]{3,2,1,0:T(8,128)(2,1)}), bf16[8,8,16,768]{3,2,1,0:T(8,128)(2,1)}) %reduce-scatter.11.cloned.1.call-update) | async-done | bytes 1572880 | tf_op jit(solution)/shard_map/reduce_scatter | solution.py:247
  731.5 9.6 fusion.22
  754.8 9.6 add_convert_fusion.1
  764.8 5.8 multiply_reduce_fusion.3
  776.4 40.3 %all-reduce.6 = (f32[768]{0:T(1024)S(1)}, f32[2,768]{1,0:T(2,128)S(1)}, f32[6,768]{1,0:T(8,128)S(1)}, f32[3072]{0:T(1024)S(1)}) all-reduce(f32[768]{0:T(1024)S(1)} %get-tuple-element.248, f32[2,768]{1,0:T(2,128)S(1)} %pad_maximum_fusion.3, f32[6,768]{1,0:T(8,128)S(1)} %stack.27, ...), channel_id=6, replica_groups=mesh['seq'=4,'clip'=8] {'seq','clip'}, use_global_device_ids=true, to_apply=%region_21.22.clone | all-reduce | flops 9984 | bytes 79872
  819.1 18.0 %reduce-scatter.15.cloned.1.call-done = f32[24,768]{1,0:T(8,128)} async-done(((f32[768,768]{1,0:T(8,128)}), f32[24,768]{1,0:T(8,128)}) %reduce-scatter.15.cloned.1.call-update) | async-done | bytes 73744 | tf_op jit(solution)/shard_map/reduce_scatter | solution.py:281
  837.2 141.8 %reduce-scatter.17.cloned.1.call-done = f32[24,3072]{1,0:T(8,128)} async-done(((f32[768,3072]{1,0:T(8,128)}), f32[24,3072]{1,0:T(8,128)}) %reduce-scatter.17.cloned.1.call-update) | async-done | bytes 294928 | tf_op jit(solution)/shard_map/reduce_scatter | solution.py:285
  979.0 141.5 %reduce-scatter.19.cloned.1.call-done = f32[96,768]{1,0:T(8,128)} async-done(((f32[3072,768]{1,0:T(8,128)}), f32[96,768]{1,0:T(8,128)}) %reduce-scatter.19.cloned.1.call-update) | async-done | bytes 294928 | tf_op jit(solution)/shard_map/reduce_scatter | solution.py:286
  1120.5 124.8 %reduce-scatter.13.cloned.1.call-done = f32[24,2304]{1,0:T(8,128)} async-done(((f32[768,2304]{1,0:T(8,128)}), f32[24,2304]{1,0:T(8,128)}) %reduce-scatter.13.cloned.1.call-update) | async-done | bytes 221200 | tf_op jit(solution)/shard_map/reduce_scatter | solution.py:280
  (279 shorter events, 113.3 us)
Async XLA Ops:
  7.2 181.5 %copy-start.11 = (bf16[8,8,16,768]{3,2,1,0:T(8,128)(2,1)S(1)}, bf16[8,8,16,768]{3,2,1,0:T(8,128)(2,1)}, u32[]{:S(2)}) copy-start(bf16[8,8,16,768]{3,2,1,0:T(8,128)(2,1)} %param.24) | copy-start | bytes 4718596
  7.2 184.8 %all-gather.8.cloned.1.call-start = ((), (), s32[]{:S(2)}) async-start(), calls=%async_computation.6 | async-start | bytes 3649536 | tf_op jit(solution)/shard_map/all_gather | solution.py:158
  7.9 297.1 %all-gather.10.cloned.1.call-start = ((), (), s32[]{:S(2)}) async-start(), calls=%async_computation.7 | async-start | bytes 7864320 | tf_op jit(solution)/shard_map/all_gather | solution.py:197
  52.6 139.4 %copy-start.30 = (f32[768]{0:T(1024)}, f32[768]{0:T(1024)S(1)}, u32[]{:S(2)}) copy-start(f32[768]{0:T(1024)S(1)} %convert_element_type.162) | copy-start | bytes 9220
  188.7 9.7 copy-start.37
  202.5 141.6 %all-gather.12.cloned.1.call-start = ((), (), s32[]{:S(2)}) async-start(), calls=%async_computation.8 | async-start | bytes 1216512 | tf_op jit(solution)/shard_map/all_gather | solution.py:159
  203.3 196.1 %all-gather.14.cloned.1.call-start = ((), (), s32[]{:S(2)}) async-start(), calls=%async_computation.9 | async-start | bytes 4866048 | tf_op jit(solution)/shard_map/all_gather | solution.py:163
  203.9 260.2 %all-gather.16.cloned.1.call-start = ((), (), s32[]{:S(2)}) async-start(), calls=%async_computation.10 | async-start | bytes 4866048 | tf_op jit(solution)/shard_map/all_gather | solution.py:164
  206.0 62.9 %collective-permute-start = (bf16[8,8,16,768]{3,2,1,0:T(8,128)(2,1)S(1)}, bf16[8,8,16,768]{3,2,1,0:T(8,128)(2,1)}, u32[]{:S(2)}, u32[]{:S(2)}) collective-permute-start(bf16[8,8,16,768]{3,2,1,0:T(8,128)(2,1)S(1)} %bitcast.180), channel_id=1, source_target_pairs={{0,8},{8,16},{16,24},{24,0},{1,9},{9,17},{17,25},{25,1},{2,10},{10... | collective-permute-start | bytes 4718600 | tf_op jit(solution)/shard_map/ppermute | solution.py:20
  206.0 79.2 %collective-permute-start.1 = (bf16[8,8,16,768]{3,2,1,0:T(8,128)(2,1)S(1)}, bf16[8,8,16,768]{3,2,1,0:T(8,128)(2,1)}, u32[]{:S(2)}, u32[]{:S(2)}) collective-permute-start(bf16[8,8,16,768]{3,2,1,0:T(8,128)(2,1)S(1)} %bitcast.181), channel_id=1, source_target_pairs={{0,24},{8,0},{16,8},{24,16},{1,25},{9,1},{17,9},{25,17},{2,26},{10... | collective-permute-start | bytes 4718600 | tf_op jit(solution)/shard_map/ppermute | solution.py:23
  268.8 24.8 %collective-permute-start.2 = (bf16[8,8,16,768]{3,2,1,0:T(8,128)(2,1)}, bf16[8,8,16,768]{3,2,1,0:T(8,128)(2,1)}, u32[]{:S(2)}, u32[]{:S(2)}) collective-permute-start(bf16[8,8,16,768]{3,2,1,0:T(8,128)(2,1)} %collective-permute-done), channel_id=1, source_target_pairs={{0,8},{8,16},{16,24},{24,0},{1,9},{9,17},{17,25},{25,1},{2,10},{10... | collective-permute-start | bytes 4718600 | tf_op jit(solution)/shard_map/ppermute | solution.py:20
  275.3 395.8 %reduce-scatter.9.cloned.1.call-start = ((), (), s32[]{:S(2)}) async-start(), calls=%async_computation.11 | async-start | bytes 7864320 | tf_op jit(solution)/shard_map/reduce_scatter | solution.py:239
  305.0 8.7 copy-start.60
  313.7 31.5 %copy-start.31 = (f32[768]{0:T(1024)S(1)}, f32[768]{0:T(1024)}, u32[]{:S(2)}) copy-start(f32[768]{0:T(1024)} %copy-done.30) | copy-start | bytes 9220
  313.7 31.5 %copy-start.48 = (pred[8,128]{1,0:T(8,128)(4,1)S(1)}, pred[8,128]{1,0:T(8,128)(4,1)}, u32[]{:S(2)}) copy-start(pred[8,128]{1,0:T(8,128)(4,1)} %copy-done.47) | copy-start | bytes 3076
  313.8 31.5 %copy-start.57 = (f32[768]{0:T(1024)S(1)}, f32[768]{0:T(1024)}, u32[]{:S(2)}) copy-start(f32[768]{0:T(1024)} %get-tuple-element.188) | copy-start | bytes 9220
  349.1 143.4 %copy-start.7 = (f32[1024,768]{1,0:T(8,128)}, f32[1024,768]{1,0:T(8,128)S(1)}, u32[]{:S(2)}) copy-start(f32[1024,768]{1,0:T(8,128)S(1)} %get-tuple-element.251) | copy-start | bytes 9437188
  349.2 50.2 %copy-start.33 = (f32[768]{0:T(1024)S(1)}, f32[768]{0:T(1024)}, u32[]{:S(2)}) copy-start(f32[768]{0:T(1024)} %get-tuple-element.192) | copy-start | bytes 9220
  349.2 50.2 %copy-start.35 = (f32[768]{0:T(1024)S(1)}, f32[768]{0:T(1024)}, u32[]{:S(2)}) copy-start(f32[768]{0:T(1024)} %get-tuple-element.187) | copy-start | bytes 9220
  349.2 50.2 %copy-start.51 = (f32[3072]{0:T(1024)S(1)}, f32[3072]{0:T(1024)}, u32[]{:S(2)}) copy-start(f32[3072]{0:T(1024)} %convert_element_type.172) | copy-start | bytes 36868
  349.2 143.4 %copy-start.25 = (f32[1024]{0:T(1024)}, f32[1024]{0:T(1024)S(1)}, u32[]{:S(2)}) copy-start(f32[1024]{0:T(1024)S(1)} %broadcast_multiply_fusion.2) | copy-start | bytes 12292
  349.7 142.9 %copy-start.28 = (f32[1024]{0:T(1024)}, f32[1024]{0:T(1024)S(1)}, u32[]{:S(2)}) copy-start(f32[1024]{0:T(1024)S(1)} %fusion.24) | copy-start | bytes 12292
  520.0 12.5 copy-start.1
  577.8 12.5 copy-start.1
  614.7 116.8 %reduce-scatter.11.cloned.1.call-start = ((), (), s32[]{:S(2)}) async-start(), calls=%async_computation.12 | async-start | bytes 7864320 | tf_op jit(solution)/shard_map/reduce_scatter | solution.py:247
  615.5 221.7 %reduce-scatter.15.cloned.1.call-start = ((), (), s32[]{:S(2)}) async-start(), calls=%async_computation.14 | async-start | bytes 2433024 | tf_op jit(solution)/shard_map/reduce_scatter | solution.py:281
  620.4 358.6 %reduce-scatter.17.cloned.1.call-start = ((), (), s32[]{:S(2)}) async-start(), calls=%async_computation.15 | async-start | bytes 9732096 | tf_op jit(solution)/shard_map/reduce_scatter | solution.py:285
  632.9 487.6 %reduce-scatter.19.cloned.1.call-start = ((), (), s32[]{:S(2)}) async-start(), calls=%async_computation.16 | async-start | bytes 9732096 | tf_op jit(solution)/shard_map/reduce_scatter | solution.py:286
  643.6 601.7 %reduce-scatter.13.cloned.1.call-start = ((), (), s32[]{:S(2)}) async-start(), calls=%async_computation.13 | async-start | bytes 7299072 | tf_op jit(solution)/shard_map/reduce_scatter | solution.py:280
  741.1 9.0 copy-start.22
  741.1 10.8 copy-start.24
  741.2 12.4 copy-start.23
  741.2 13.2 %copy-start.50 = (f32[768]{0:T(1024)S(1)}, f32[768]{0:T(1024)}, u32[]{:S(2)}) copy-start(f32[768]{0:T(1024)} %get-tuple-element.230) | copy-start | bytes 9220
  741.2 12.4 copy-start.27
  741.2 13.1 %copy-start.55 = (f32[768]{0:T(1024)S(1)}, f32[768]{0:T(1024)}, u32[]{:S(2)}) copy-start(f32[768]{0:T(1024)} %get-tuple-element.180) | copy-start | bytes 9220
  741.2 13.1 %copy-start.54 = (f32[768]{0:T(1024)S(1)}, f32[768]{0:T(1024)}, u32[]{:S(2)}) copy-start(f32[768]{0:T(1024)} %get-tuple-element.184) | copy-start | bytes 9220
  741.2 13.1 %copy-start.17 = (bf16[2,4,128,768]{2,3,1,0:T(8,128)(2,1)S(1)}, bf16[2,4,128,768]{2,3,1,0:T(8,128)(2,1)}, u32[]{:S(2)}) copy-start(bf16[2,4,128,768]{2,3,1,0:T(8,128)(2,1)} %get-tuple-element.102) | copy-start | bytes 4718596
  741.2 13.4 %copy-start.56 = (f32[768]{0:T(1024)S(1)}, f32[768]{0:T(1024)}, u32[]{:S(2)}) copy-start(f32[768]{0:T(1024)} %get-tuple-element.186) | copy-start | bytes 9220
  754.7 9.7 copy-start.19
  754.7 10.0 copy-start.12
  754.7 10.0 copy-start.20
  754.7 10.0 copy-start.32
  754.7 10.0 copy-start.38
  754.7 10.0 copy-start.40
  754.7 10.0 copy-start.42
  754.7 10.0 copy-start.49
  754.8 10.0 copy-start.58
  754.8 10.0 copy-start.59
  (36 other events, 141.3 us)
Sparse Core Ops, SparseCore 0:
  10.9 62.7 all-gather.7
  202.7 76.9 all-gather.9
  282.5 51.3 all-gather.11
  336.7 62.5 all-gather.13
  402.1 61.9 all-gather.15
  614.8 56.1 reduce-scatter.8
  673.6 57.9 reduce-scatter.10
  737.4 99.7 reduce-scatter.14
  843.6 135.2 reduce-scatter.16
  985.3 135.1 reduce-scatter.18
  1126.7 118.4 reduce-scatter.12
